TPU v7x, 32 devices: a whole 2x2x4 slice. The times are simulated.
32 devices in a mesh: blk: 8 (over z, y), wide: 4 (over x, core).
Axes of the slice: x: 2, y: 2, z: 4, core: 2. Of those that a mesh axis runs over, the one named last changes fastest.
Arguments:
- query_rows: bfloat16 [4, 1024, 1536], P('wide', 'blk'), may hold values from -40 to 40
- key_rows: bfloat16 [4, 1024, 1536], P('wide', 'blk'), may hold values from -6 to 6
- value_rows: bfloat16 [4, 1024, 1536], P('wide', 'blk'), may hold values from -6 to 6
- patch_index: int32 [4, 1024], P('wide', 'blk'), may hold values from 0 to 4095, as said below
- live_count: int32 [4, 8], P('wide', 'blk'), may hold values from 64 to 128, as said below
- slopes: float32 [12], replicated, may hold values from 0.003 to 0.15
- out_weight: bfloat16 [1536, 1536], P('wide'), may hold values from -0.15625 to 0.15625
- out_grad: bfloat16 [4, 1024, 1536], P('wide', 'blk'), may hold values from -6 to 6
Outputs:
- layer_out: bfloat16 [4, 1024, 1536], P('wide', 'blk')
- grad_query: bfloat16 [4, 1024, 1536], P('wide', 'blk')
- grad_key: bfloat16 [4, 1024, 1536], P('wide', 'blk')
- grad_value: bfloat16 [4, 1024, 1536], P('wide', 'blk')
- grad_weight: float32 [1536, 1536], P('wide')
Inputs may be any that keep to these rules, and one draw needn't show every extreme that they name: `patch_index`: within a slab b, the slots hold distinct patch numbers of the range b * 512 to (b + 1) * 512 - 1 in increasing order; slots beyond the live count hold such numbers too. `live_count`: every crop has a slab with exactly 128 live slots; the live slots of a slab are its first ones.
All inputs are finite; a program needn't handle non-finite values.
Results may differ from a plain program's by a relative error of at most 0.015.
Values may be sent and summed in bfloat16 or wider, within the bound.
A program may use at most 128 MiB of HBM per device.

v0:
```python
import jax
import jax.numpy as jnp
from jax import lax
from jax.sharding import PartitionSpec as P

HEADS = 12
HEAD_DIM = 128
SIDE = 32
MASKED = -1e30


def coordinates(index):
    return (index % SIDE, index // SIDE % SIDE, index // (SIDE * SIDE))


def spacing(row_index, col_index):
    row_x, row_y, row_z = coordinates(row_index)
    col_x, col_y, col_z = coordinates(col_index)
    distance = (
        jnp.abs(row_x[:, None] - col_x[None, :])
        + jnp.abs(row_y[:, None] - col_y[None, :])
        + jnp.abs(row_z[:, None] - col_z[None, :])
    )
    return distance.astype(jnp.float32)


def biased_scores(query_heads, key_heads, row_index, col_index, key_live, slopes):
    scaling = HEAD_DIM ** (-0.5)
    scores = (
        jnp.einsum("qhd,khd->hqk", query_heads, key_heads, preferred_element_type=jnp.float32)
        * scaling
    )
    scores = scores - slopes[:, None, None] * spacing(row_index, col_index)[None]
    return jnp.where(key_live[None, None, :], scores, MASKED)


def body(query_rows, key_rows, value_rows, patch_index, live_count, slopes, out_weight, out_grad):
    slot_count = query_rows.shape[1]
    inner_width = query_rows.shape[2]
    blocks = lax.axis_size("blk")
    extent = slot_count * blocks
    scaling = HEAD_DIM ** (-0.5)
    key_all, value_all, index_all, count_all = (
        lax.all_gather(key_rows, "blk", axis=1, tiled=True),
        lax.all_gather(value_rows, "blk", axis=1, tiled=True),
        lax.all_gather(patch_index, "blk", axis=1, tiled=True),
        lax.all_gather(live_count, "blk", axis=1, tiled=True),
    )
    weight_all = lax.all_gather(out_weight, "wide", axis=0, tiled=True)
    position = jnp.arange(extent, dtype=jnp.int32)
    key_live = position % slot_count < jnp.repeat(count_all[0], slot_count)
    query_live = jnp.arange(slot_count, dtype=jnp.int32) < live_count[0, 0]
    query_heads = query_rows[0].reshape(slot_count, HEADS, HEAD_DIM)
    key_heads = key_all[0].reshape(extent, HEADS, HEAD_DIM)
    value_heads = value_all[0].reshape(extent, HEADS, HEAD_DIM)
    scores = biased_scores(query_heads, key_heads, patch_index[0], index_all[0], key_live, slopes)
    row_max = jnp.max(scores, axis=2, keepdims=True)
    row_lse = row_max + jnp.log(jnp.sum(jnp.exp(scores - row_max), axis=2, keepdims=True))
    attn_prob = jnp.exp(scores - row_lse)
    prob_low = attn_prob.astype(jnp.bfloat16)
    attended = jnp.einsum(
        "hqk,khd->qhd", prob_low, value_heads, preferred_element_type=jnp.float32
    ).reshape(slot_count, inner_width)
    attended = jnp.where(query_live[:, None], attended, 0.0).astype(jnp.bfloat16)
    layer_out = jnp.dot(attended, weight_all, preferred_element_type=jnp.float32).astype(
        jnp.bfloat16
    )
    grad_att = jnp.einsum("qo,io->qi", out_grad[0], weight_all, preferred_element_type=jnp.float32)
    grad_att = jnp.where(query_live[:, None], grad_att, 0.0).astype(jnp.bfloat16)
    grad_heads = grad_att.reshape(slot_count, HEADS, HEAD_DIM)
    grad_prob = jnp.einsum(
        "qhd,khd->hqk", grad_heads, value_heads, preferred_element_type=jnp.float32
    )
    row_delta = jnp.sum(attn_prob * grad_prob, axis=2, keepdims=True)
    grad_score = (attn_prob * (grad_prob - row_delta)).astype(jnp.bfloat16)
    grad_query = (
        jnp.einsum("hqk,khd->qhd", grad_score, key_heads, preferred_element_type=jnp.float32)
        * scaling
    )
    grad_query = grad_query.reshape(slot_count, inner_width).astype(jnp.bfloat16)
    key_part = (
        jnp.einsum("hqk,qhd->khd", grad_score, query_heads, preferred_element_type=jnp.float32)
        * scaling
    )
    value_part = jnp.einsum(
        "hqk,qhd->khd", prob_low, grad_heads, preferred_element_type=jnp.float32
    )
    stacked = lax.psum_scatter(
        jnp.concatenate(
            [
                key_part.reshape(slot_count * lax.axis_size("blk"), inner_width),
                value_part.reshape(slot_count * lax.axis_size("blk"), inner_width),
            ],
            axis=1,
        ).astype(jnp.bfloat16),
        "blk",
        scatter_dimension=0,
        tiled=True,
    ).astype(jnp.float32)
    grad_key = stacked[:, :inner_width]
    grad_value = stacked[:, inner_width:]
    weight_share = lax.psum_scatter(
        jnp.einsum("qi,qo->io", attended, out_grad[0], preferred_element_type=jnp.float32).astype(
            jnp.bfloat16
        ),
        "wide",
        scatter_dimension=0,
        tiled=True,
    )
    grad_weight = lax.psum(weight_share, "blk").astype(jnp.float32)
    return (
        layer_out[None],
        grad_query[None],
        grad_key.astype(jnp.bfloat16)[None],
        grad_value.astype(jnp.bfloat16)[None],
        grad_weight,
    )


def solution(mesh):
    placed = (
        P("wide", "blk", None),
        P("wide", "blk", None),
        P("wide", "blk", None),
        P("wide", "blk"),
        P("wide", "blk"),
        P(),
        P("wide", None),
        P("wide", "blk", None),
    )
    return jax.shard_map(
        body,
        mesh=mesh,
        in_specs=placed,
        out_specs=(
            P("wide", "blk", None),
            P("wide", "blk", None),
            P("wide", "blk", None),
            P("wide", "blk", None),
            P("wide", None),
        ),
        check_vma=False,
    )
```

profile of v0, /device:TPU:0, one launch (start us, length us, event | category | flops | bytes accessed | tf_op | source)
XLA Modules:
  0.0 438.7 jit_solution(17372420992421060902)
XLA Ops:
  8.0 1.9 copy.25
  10.0 0.7 all-gather.8.cloned.1.call-update
  11.3 1.2 dynamic-slice
  13.3 13.2 %all-reduce = s32[8]{0:T(128)S(1)} all-reduce(s32[8]{0:T(128)S(1)} %bitcast_dynamic-update-slice_fusion), channel_id=1, replica_groups=mesh['blk'=8,'wide'=4] {'blk'}, use_global_device_ids=true, to_apply=%add | all-reduce | flops 8 | bytes 64
  26.5 1.9 copy.24
  28.4 17.8 %all_gather.17 = s32[1,1024]{1,0:T(1,128)S(1)} all-gather(s32[1,128]{1,0:T(1,128)} %param.11), channel_id=1, replica_groups=mesh['blk'=8,'wide'=4] {'blk'}, dimensions={1}, use_global_device_ids=true | all-gather | bytes 4608 | tf_op jit(solution)/shard_map/all_gather | solution.py:46
  47.1 1.1 add_convert_fusion
  48.2 25.3 %all-gather.6.cloned.1.call-done = bf16[1,1024,1536]{2,1,0:T(8,128)(2,1)} async-done(((bf16[1,128,1536]{2,1,0:T(8,128)(2,1)}), bf16[1,1024,1536]{2,1,0:T(8,128)(2,1)}) %all-gather.6.cloned.1.call-update) | async-done | bytes 3145744 | tf_op jit(solution)/shard_map/all_gather | solution.py:45
  73.5 3.2 copy.28
  76.7 61.1 %all-gather.4.cloned.1.call-done = bf16[1,1024,1536]{1,2,0:T(8,128)(2,1)} async-done(((bf16[1,128,1536]{1,2,0:T(8,128)(2,1)}), bf16[1,1024,1536]{1,2,0:T(8,128)(2,1)}) %all-gather.4.cloned.1.call-update) | async-done | bytes 3145744 | tf_op jit(solution)/shard_map/all_gather | solution.py:44
  137.8 4.0 fusion.19
  141.8 1.5 exponential_reduce_fusion
  143.3 2.2 fusion.7
  145.5 3.5 convolution_convert_fusion
  149.1 25.9 %all-gather.8.cloned.1.call-done = bf16[1536,1536]{1,0:T(8,128)(2,1)} async-done(((bf16[384,1536]{1,0:T(8,128)(2,1)}), bf16[1536,1536]{1,0:T(8,128)(2,1)}) %all-gather.8.cloned.1.call-update) | async-done | bytes 4718608 | tf_op jit(solution)/shard_map/all_gather | solution.py:49
  175.0 4.0 fusion.1
  179.3 6.4 %multiply_reduce_fusion = (f32[12,128]{1,0:T(8,128)S(1)}, f32[12,128,1024]{2,1,0:T(8,128)S(1)}) fusion(f32[12,128,1024]{2,1,0:T(8,128)} %copy-done.1, f32[12,128]{1,0:T(8,128)S(1)} %log_add_fusion, bf16[128,12,128]{0,2,1:T(8,128)(2,1)S(1)} %bitcast.86, bf16[1024,12,128]{0,2,1:T(8,128)(2,1)} %bitcast.83), kind=kOutput, calls=%fused_computation.4 | convolution fusion | flops 407370240 | bytes 16134144 | tf_op jit(solution)/shard_map/qhd,khd->hqk/dot_general | solution.py:71
  185.7 2.6 multiply_convert_fusion.1
  188.3 37.0 %reduce-scatter.5.cloned.1.call-done = bf16[384,1536]{1,0:T(8,128)(2,1)} async-done(((bf16[1536,1536]{1,0:T(8,128)(2,1)}), bf16[384,1536]{1,0:T(8,128)(2,1)}) %reduce-scatter.5.cloned.1.call-update) | async-done | bytes 1179664 | tf_op jit(solution)/shard_map/reduce_scatter | solution.py:102
  225.6 5.9 %convolution_convert_fusion.2 = bf16[12,128,1024]{2,1,0:T(8,128)(2,1)} fusion(bf16[128,12,128]{0,2,1:T(8,128)(2,1)} %bitcast.87, f32[12,128,1024]{2,1,0:T(8,128)} %copy-done.1, f32[12,128]{1,0:T(8,128)S(1)} %log_add_fusion), kind=kOutput, calls=%fused_computation.13 | convolution fusion | flops 407371776 | bytes 9836544 | tf_op jit(solution)/shard_map/hqk,qhd->khd/dot_general | solution.py:85
  231.4 4.9 %copy.34 = bf16[1024,1536]{1,0:T(8,128)(2,1)} copy(bf16[1024,1536]{0,1:T(8,128)(2,1)} %bitcast.85) | data formatting | bytes 6291456 | tf_op jit(solution)/shard_map/reshape | solution.py:92
  236.3 3.7 multiply_convert_fusion
  240.0 4.7 %copy.33 = bf16[1024,1536]{1,0:T(8,128)(2,1)} copy(bf16[1024,1536]{0,1:T(8,128)(2,1)} %bitcast.84) | data formatting | bytes 6291456 | tf_op jit(solution)/shard_map/reshape | solution.py:91
  244.7 6.2 %pad_maximum_fusion = bf16[1024,3072]{1,0:T(8,128)(2,1)} fusion(bf16[1024,1536]{1,0:T(8,128)(2,1)} %copy.34, bf16[1024,1536]{1,0:T(8,128)(2,1)} %copy.33), kind=kLoop, calls=%fused_computation.1 | loop fusion | flops 12582912 | bytes 12582912 | tf_op jit(solution)/shard_map/concatenate | solution.py:89
  250.9 1.9 copy.29
  252.8 3.6 fusion.3
  256.4 1.9 copy.35
  258.4 4.1 fusion.2
  262.4 46.7 %all-reduce.3.cloned.1.call-done = bf16[384,1536]{1,0:T(8,128)(2,1)} async-done(((bf16[384,1536]{1,0:T(8,128)(2,1)}), bf16[384,1536]{1,0:T(8,128)(2,1)}) %all-reduce.3.cloned.1.call-update) | async-done | bytes 1179664 | tf_op jit(solution)/shard_map/psum | solution.py:110
  309.1 3.0 convert_element_type.65
  312.1 117.8 %reduce-scatter.3.cloned.1.call-done = bf16[128,3072]{1,0:T(8,128)(2,1)} async-done(((bf16[1024,3072]{1,0:T(8,128)(2,1)}), bf16[128,3072]{1,0:T(8,128)(2,1)}) %reduce-scatter.3.cloned.1.call-update) | async-done | bytes 786448 | tf_op jit(solution)/shard_map/reduce_scatter | solution.py:88
  429.8 2.0 slice_bitcast_fusion
  (37 shorter events, 2.9 us)
Async XLA Ops:
  7.2 138.3 %copy-start = (bf16[1,128,1536]{2,1,0:T(8,128)(2,1)S(1)}, bf16[1,128,1536]{2,1,0:T(8,128)(2,1)}, u32[]{:S(2)}) copy-start(bf16[1,128,1536]{2,1,0:T(8,128)(2,1)} %param.15) | copy-start | bytes 1179652
  7.2 130.6 %copy-start.5 = (f32[12]{0:T(128)S(1)}, f32[12]{0:T(128)}, u32[]{:S(2)}) copy-start(f32[12]{0:T(128)} %param.13) | copy-start | bytes 148
  7.2 66.3 %all-gather.6.cloned.1.call-start = ((), (), s32[]{:S(2)}) async-start(), calls=%async_computation.3 | async-start | bytes 3538944 | tf_op jit(solution)/shard_map/all_gather | solution.py:45
  7.9 129.9 %all-gather.4.cloned.1.call-start = ((), (), s32[]{:S(2)}) async-start(), calls=%async_computation.2 | async-start | bytes 3538944 | tf_op jit(solution)/shard_map/all_gather | solution.py:44
  9.9 165.1 %all-gather.8.cloned.1.call-start = ((), (), s32[]{:S(2)}) async-start(), calls=%async_computation.4 | async-start | bytes 5898240 | tf_op jit(solution)/shard_map/all_gather | solution.py:49
  10.6 214.7 %reduce-scatter.5.cloned.1.call-start = ((), (), s32[]{:S(2)}) async-start(), calls=%async_computation.6 | async-start | bytes 5898240 | tf_op jit(solution)/shard_map/reduce_scatter | solution.py:102
  76.6 66.6 %copy-start.3 = (bf16[1,1024,1536]{1,2,0:T(8,128)(2,1)}, bf16[1,1024,1536]{1,2,0:T(8,128)(2,1)S(1)}, u32[]{:S(2)}) copy-start(bf16[1,1024,1536]{1,2,0:T(8,128)(2,1)S(1)} %copy.28) | copy-start | bytes 9437188
  141.8 3.7 copy-start.1
  149.0 160.0 %all-reduce.3.cloned.1.call-start = ((), (), s32[]{:S(2)}) async-start(), calls=%async_computation.7 | async-start | bytes 2359296 | tf_op jit(solution)/shard_map/psum | solution.py:110
  179.0 6.7 %slice-start = ((s8[6291456]{0:T(1024)(128)(4,1)}), s8[2097152]{0:T(1024)(128)(4,1)S(1)}, s32[]{:S(2)}) async-start(s8[6291456]{0:T(1024)(128)(4,1)} %bitcast.80), calls=%async_computation.8 | async-start | bytes 4194304
  179.3 6.4 %copy-start.4 = (bf16[128,1536]{0,1:T(8,128)(2,1)}, bf16[128,1536]{0,1:T(8,128)(2,1)S(1)}, u32[]{:S(2)}) copy-start(bf16[128,1536]{0,1:T(8,128)(2,1)S(1)} %copy.30) | copy-start | bytes 1179652
  179.3 6.4 %slice-start.1 = ((s8[6291456]{0:T(1024)(128)(4,1)}), s8[4194304]{0:T(1024)(128)(4,1)S(1)}, s32[]{:S(2)}) async-start(s8[6291456]{0:T(1024)(128)(4,1)} %bitcast.80), calls=%async_computation.9 | async-start | bytes 8388608
  225.3 11.0 %copy-start.2 = (bf16[12,128,1024]{2,1,0:T(8,128)(2,1)S(1)}, bf16[12,128,1024]{2,1,0:T(8,128)(2,1)}, u32[]{:S(2)}) copy-start(bf16[12,128,1024]{2,1,0:T(8,128)(2,1)} %multiply_convert_fusion.1) | copy-start | bytes 9437188
  225.3 204.5 %reduce-scatter.3.cloned.1.call-start = ((), (), s32[]{:S(2)}) async-start(), calls=%async_computation.5 | async-start | bytes 7077888 | tf_op jit(solution)/shard_map/reduce_scatter | solution.py:88
Sparse Core Ops, SparseCore 0:
  10.2 63.2 all-gather.5
  76.1 61.6 all-gather.3
  139.4 35.6 all-gather.7
  177.4 47.8 reduce-scatter.4
  229.0 79.9 all-reduce.2
  312.5 117.2 reduce-scatter.2
where the time goes:
time: 439 us
  waiting for transfers between devices  315 us (72%)
  matrix products  37.3 us (8%)
  blocking collectives  31 us (7%)
  local copies, waits for them, and re-layouts  24.6 us (6%)
  other arithmetic  15.2 us (3%)
  between operations  14.9 us (3%)
    reduce_scatter x1, waiting for transfers between devices, body(): lax.psum_scatter(jnp.concatenate([key_part.reshape(slot_count * lax.axis_...  118 us
    all_gather x1, waiting for transfers between devices, body(): lax.all_gather(key_rows, 'blk', axis=1, tiled=True)  61.1 us
    psum x1, waiting for transfers between devices, body(): grad_weight = lax.psum(weight_share, 'blk').astype(jnp.float32)  46.7 us
    reduce_scatter x1, waiting for transfers between devices, body(): lax.psum_scatter(jnp.einsum('qi,qo->io', attended, out_grad[0], preferred...  37 us
    all_gather x1, waiting for transfers between devices, body(): weight_all = lax.all_gather(out_weight, 'wide', axis=0, tiled=True)  25.9 us
    all_gather x1, waiting for transfers between devices, body(): lax.all_gather(value_rows, 'blk', axis=1, tiled=True)  25.3 us
    all_gather x1, blocking collectives, body(): lax.all_gather(patch_index, 'blk', axis=1, tiled=True)  17.8 us
    unnamed x1, blocking collectives  13.2 us
  transfers between devices with their start and end apart: 6, of which 6 were waited for; matrix products, arithmetic and copies ran while one was open for 17% of the time, Pallas kernels for 0%

commit v1 on v0

--- a/solution.py
+++ b/solution.py
@@ -46,7 +46,12 @@
         lax.all_gather(patch_index, "blk", axis=1, tiled=True),
         lax.all_gather(live_count, "blk", axis=1, tiled=True),
     )
-    weight_all = lax.all_gather(out_weight, "wide", axis=0, tiled=True)
+    ring = [out_weight]
+    for hop in range(3):
+        ring.append(lax.ppermute(ring[-1], "wide", [(dev, (dev + 1) % 4) for dev in range(4)]))
+    weight_all = jnp.roll(
+        jnp.concatenate(ring[::-1], axis=0), (lax.axis_index("wide") + 1) * ring[0].shape[0], axis=0
+    )
     position = jnp.arange(extent, dtype=jnp.int32)
     key_live = position % slot_count < jnp.repeat(count_all[0], slot_count)
     query_live = jnp.arange(slot_count, dtype=jnp.int32) < live_count[0, 0]

time: 439 us -> 448 us (1.021)
  local copies, waits for them, and re-layouts: 24.6 us -> 37.1 us
  matrix products: 37.3 us -> 32.3 us
    ppermute x0 -> x3, waiting for transfers between devices: none -> 72.7 us  [body(): lax.ppermute(ring[-1], 'wide', [(dev, (dev + 1) % 4) for dev in range(4)])]
    reduce_scatter x1, waiting for transfers between devices: 37 us -> 0.02 us  [body(): lax.psum_scatter(jnp.einsum('qi,qo->io', attended, out_grad[0], preferred...]
    all_gather x1, waiting for transfers between devices: 61.1 us -> 30.3 us  [body(): lax.all_gather(key_rows, 'blk', axis=1, tiled=True)]
    all_gather x1, waiting for transfers between devices: 25.3 us -> 53 us  [body(): lax.all_gather(value_rows, 'blk', axis=1, tiled=True)]
    all_gather x1 -> x0, waiting for transfers between devices: 25.9 us -> none  [body(): weight_all = lax.all_gather(out_weight, 'wide', axis=0, tiled=True)]
    unnamed x22 -> x39, local copies, waits for them, and re-layouts: 7.7 us -> 22.4 us
  transfers between devices with their start and end apart: 6 -> 8, of which waited for: 6 -> 7; matrix products, arithmetic and copies ran while one was open for 17% -> 13% of each run, Pallas kernels for 0% -> 0%
where the time goes in v1:
time: 448 us; the launch traced here: 447 us
  waiting for transfers between devices  317 us (71%)
  local copies, waits for them, and re-layouts  37.1 us (8%)
  matrix products  32.3 us (7%)
  blocking collectives  31.1 us (7%)
  between operations  14.7 us (3%)
  other arithmetic  14.2 us (3%)
    reduce_scatter x1, waiting for transfers between devices, body(): lax.psum_scatter(jnp.concatenate([key_part.reshape(slot_count * lax.axis_...  118 us
    ppermute x3, waiting for transfers between devices, body(): lax.ppermute(ring[-1], 'wide', [(dev, (dev + 1) % 4) for dev in range(4)])  72.7 us
    all_gather x1, waiting for transfers between devices, body(): lax.all_gather(value_rows, 'blk', axis=1, tiled=True)  53 us
    psum x1, waiting for transfers between devices, body(): grad_weight = lax.psum(weight_share, 'blk').astype(jnp.float32)  42.8 us
    all_gather x1, waiting for transfers between devices, body(): lax.all_gather(key_rows, 'blk', axis=1, tiled=True)  30.3 us
    unnamed x39, local copies, waits for them, and re-layouts  22.4 us
    all_gather x1, blocking collectives, body(): lax.all_gather(patch_index, 'blk', axis=1, tiled=True)  18 us
    unnamed x1, blocking collectives  13.2 us
  transfers between devices with their start and end apart: 8, of which 7 were waited for; matrix products, arithmetic and copies ran while one was open for 13% of the time, Pallas kernels for 0%

profile of v1, /device:TPU:0, one launch (start us, length us, event | category | flops | bytes accessed | tf_op | source)
XLA Modules:
  0.0 447.3 jit_solution(14106392855568644347)
XLA Ops:
  7.2 2.0 copy.23
  12.6 13.2 %all-reduce = s32[8]{0:T(128)S(1)} all-reduce(s32[8]{0:T(128)S(1)} %bitcast_dynamic-update-slice_fusion), channel_id=1, replica_groups=mesh['blk'=8,'wide'=4] {'blk'}, use_global_device_ids=true, to_apply=%add | all-reduce | flops 8 | bytes 64
  27.0 18.0 %all_gather.14 = s32[1,1024]{1,0:T(1,128)S(1)} all-gather(s32[1,128]{1,0:T(1,128)} %param.11), channel_id=1, replica_groups=mesh['blk'=8,'wide'=4] {'blk'}, dimensions={1}, use_global_device_ids=true | all-gather | bytes 4608 | tf_op jit(solution)/shard_map/all_gather | solution.py:46
  46.1 30.3 %all-gather.3.cloned.1.call-done = bf16[1,1024,1536]{1,2,0:T(8,128)(2,1)} async-done(((bf16[1,128,1536]{1,2,0:T(8,128)(2,1)}), bf16[1,1024,1536]{1,2,0:T(8,128)(2,1)}) %all-gather.3.cloned.1.call-update) | async-done | bytes 3145744 | tf_op jit(solution)/shard_map/all_gather | solution.py:44
  76.5 3.8 fusion.33
  80.3 2.6 copy-done.2
  82.9 1.4 exponential_reduce_fusion
  84.3 53.0 %all-gather.5.cloned.1.call-done = bf16[1,1024,1536]{2,1,0:T(8,128)(2,1)} async-done(((bf16[1,128,1536]{2,1,0:T(8,128)(2,1)}), bf16[1,1024,1536]{2,1,0:T(8,128)(2,1)}) %all-gather.5.cloned.1.call-update) | async-done | bytes 3145744 | tf_op jit(solution)/shard_map/all_gather | solution.py:45
  137.3 3.2 copy.26
  140.5 4.8 %fusion.22 = (bf16[128,12,128]{0,2,1:T(8,128)(2,1)S(1)}, bf16[12,128,128]{1,2,0:T(8,128)(2,1)}) fusion(pred[128]{0:T(512)(128)(4,1)S(1)} %iota_compare_fusion, bf16[1024,12,128]{0,2,1:T(8,128)(2,1)S(1)} %bitcast.86, f32[12,128,1024]{2,1,0:T(8,128)} %copy-done.2, f32[12,128]{1,0:T(8,128)S(1)} %log_add_fusion), kind=kOutput, calls=%fused_computation.24 | convolution fusion | flops 405995520 | bytes 10229888 | tf_op jit(solution)/shard_map/hqk,khd->qhd/dot_general | solution.py:66
  145.3 3.5 convolution_convert_fusion
  149.0 15.8 %collective-permute-done = bf16[384,1536]{1,0:T(8,128)(2,1)S(1)} collective-permute-done((bf16[384,1536]{1,0:T(8,128)(2,1)}, bf16[384,1536]{1,0:T(8,128)(2,1)S(1)}, u32[]{:S(2)}, u32[]{:S(2)}) %collective-permute-start) | collective-permute-done | bytes 1179680 | tf_op jit(solution)/shard_map/ppermute | solution.py:51
  165.8 40.9 %collective-permute-done.1 = bf16[384,1536]{1,0:T(8,128)(2,1)} collective-permute-done((bf16[384,1536]{1,0:T(8,128)(2,1)S(1)}, bf16[384,1536]{1,0:T(8,128)(2,1)}, u32[]{:S(2)}, u32[]{:S(2)}) %collective-permute-start.1) | collective-permute-done | bytes 1179680 | tf_op jit(solution)/shard_map/ppermute | solution.py:51
  206.8 15.9 %collective-permute-done.2 = bf16[384,1536]{1,0:T(8,128)(2,1)} collective-permute-done((bf16[384,1536]{1,0:T(8,128)(2,1)}, bf16[384,1536]{1,0:T(8,128)(2,1)}, u32[]{:S(2)}, u32[]{:S(2)}) %collective-permute-start.2) | collective-permute-done | bytes 1179680 | tf_op jit(solution)/shard_map/ppermute | solution.py:51
  224.1 1.4 constant_dynamic-update-slice_fusion.6
  229.9 1.4 fusion.8
  231.3 3.3 copy-done.6
  234.6 1.4 slice-done.1
  236.1 2.1 multiply_reduce_fusion
  238.2 1.4 multiply_convert_fusion.1
  239.9 5.6 %convolution_convert_fusion.1 = bf16[12,128,1024]{2,1,0:T(8,128)(2,1)} fusion(bf16[128,12,128]{0,2,1:T(8,128)(2,1)S(1)} %bitcast.94, f32[12,128,1024]{2,1,0:T(8,128)} %copy-done.2, f32[12,128]{1,0:T(8,128)S(1)} %log_add_fusion), kind=kOutput, calls=%fused_computation.17 | convolution fusion | flops 407371776 | bytes 9836544 | tf_op jit(solution)/shard_map/hqk,qhd->khd/dot_general | solution.py:90
  245.5 4.7 %copy.30 = bf16[1024,1536]{1,0:T(8,128)(2,1)} copy(bf16[1024,1536]{0,1:T(8,128)(2,1)} %bitcast.89) | data formatting | bytes 6291456 | tf_op jit(solution)/shard_map/reshape | solution.py:97
  250.2 2.6 multiply_convert_fusion
  252.8 4.7 %copy.29 = bf16[1024,1536]{1,0:T(8,128)(2,1)} copy(bf16[1024,1536]{0,1:T(8,128)(2,1)} %bitcast.88) | data formatting | bytes 6291456 | tf_op jit(solution)/shard_map/reshape | solution.py:96
  257.6 6.2 %pad_maximum_fusion = bf16[1024,3072]{1,0:T(8,128)(2,1)} fusion(bf16[1024,1536]{1,0:T(8,128)(2,1)} %copy.30, bf16[1024,1536]{1,0:T(8,128)(2,1)} %copy.29), kind=kLoop, calls=%fused_computation.1 | loop fusion | flops 12582912 | bytes 12582912 | tf_op jit(solution)/shard_map/concatenate | solution.py:94
  263.8 3.7 fusion.17
  267.5 1.9 copy.31
  270.5 4.7 %fusion.14 = bf16[1,128,1536]{2,1,0:T(8,128)(2,1)} fusion(bf16[128,1536]{0,1:T(8,128)(2,1)S(1)} %fusion.21, bf16[3072,1536]{1,0:T(8,128)(2,1)} %copy-done.6, s32[]{:T(128)S(6)} %select_n.113), kind=kOutput, calls=%fused_computation.16 | convolution fusion | flops 604176384 | bytes 5505028 | tf_op jit(solution)/shard_map/dot_general | solution.py:70
  275.2 42.8 %all-reduce.3.cloned.1.call-done = bf16[384,1536]{1,0:T(8,128)(2,1)} async-done(((bf16[384,1536]{1,0:T(8,128)(2,1)}), bf16[384,1536]{1,0:T(8,128)(2,1)}) %all-reduce.3.cloned.1.call-update) | async-done | bytes 1179664 | tf_op jit(solution)/shard_map/psum | solution.py:115
  318.0 3.0 convert_element_type.69
  321.0 117.8 %reduce-scatter.3.cloned.1.call-done = bf16[128,3072]{1,0:T(8,128)(2,1)} async-done(((bf16[1024,3072]{1,0:T(8,128)(2,1)}), bf16[128,3072]{1,0:T(8,128)(2,1)}) %reduce-scatter.3.cloned.1.call-update) | async-done | bytes 786448 | tf_op jit(solution)/shard_map/reduce_scatter | solution.py:93
  438.7 2.0 slice_bitcast_fusion
  (57 shorter events, 13.3 us)
Async XLA Ops:
  7.2 138.2 %copy-start = (bf16[1,128,1536]{2,1,0:T(8,128)(2,1)S(1)}, bf16[1,128,1536]{2,1,0:T(8,128)(2,1)}, u32[]{:S(2)}) copy-start(bf16[1,128,1536]{2,1,0:T(8,128)(2,1)} %param.15) | copy-start | bytes 1179652
  7.2 69.3 %all-gather.3.cloned.1.call-start = ((), (), s32[]{:S(2)}) async-start(), calls=%async_computation.2 | async-start | bytes 3538944 | tf_op jit(solution)/shard_map/all_gather | solution.py:44
  9.2 128.1 %all-gather.5.cloned.1.call-start = ((), (), s32[]{:S(2)}) async-start(), calls=%async_computation.3 | async-start | bytes 3538944 | tf_op jit(solution)/shard_map/all_gather | solution.py:45
  10.0 229.6 %reduce-scatter.5.cloned.1.call-start = ((), (), s32[]{:S(2)}) async-start(), calls=%async_computation.5 | async-start | bytes 5898240 | tf_op jit(solution)/shard_map/reduce_scatter | solution.py:107
  27.0 57.3 %copy-start.9 = (bf16[1,128,1536]{1,2,0:T(8,128)(2,1)}, bf16[1,128,1536]{1,2,0:T(8,128)(2,1)S(1)}, u32[]{:S(2)}) copy-start(bf16[1,128,1536]{1,2,0:T(8,128)(2,1)S(1)} %copy.22) | copy-start | bytes 1179652
  80.3 2.6 copy-start.2
  148.9 169.1 %all-reduce.3.cloned.1.call-start = ((), (), s32[]{:S(2)}) async-start(), calls=%async_computation.6 | async-start | bytes 2359296 | tf_op jit(solution)/shard_map/psum | solution.py:115
  148.9 15.9 %collective-permute-start = (bf16[384,1536]{1,0:T(8,128)(2,1)}, bf16[384,1536]{1,0:T(8,128)(2,1)S(1)}, u32[]{:S(2)}, u32[]{:S(2)}) collective-permute-start(bf16[384,1536]{1,0:T(8,128)(2,1)} %param.14), channel_id=1, source_target_pairs={{0,1},{1,2},{2,3},{3,0},{4,5},{5,6},{6,7},{7,4},{8,9},{9,10},{10,1... | collective-permute-start | bytes 3538952 | tf_op jit(solution)/shard_map/ppermute | solution.py:51
  164.8 1.0 copy-start.4
  165.8 40.9 %collective-permute-start.1 = (bf16[384,1536]{1,0:T(8,128)(2,1)S(1)}, bf16[384,1536]{1,0:T(8,128)(2,1)}, u32[]{:S(2)}, u32[]{:S(2)}) collective-permute-start(bf16[384,1536]{1,0:T(8,128)(2,1)S(1)} %collective-permute-done), channel_id=1, source_target_pairs={{0,1},{1,2},{2,3},{3,0},{4,5},{5,6},{6,7},{7,4},{8,9},{9,10},{10,1... | collective-permute-start | bytes 3538952 | tf_op jit(solution)/shard_map/ppermute | solution.py:51
  206.8 15.9 %collective-permute-start.2 = (bf16[384,1536]{1,0:T(8,128)(2,1)}, bf16[384,1536]{1,0:T(8,128)(2,1)}, u32[]{:S(2)}, u32[]{:S(2)}) collective-permute-start(bf16[384,1536]{1,0:T(8,128)(2,1)} %collective-permute-done.1), channel_id=1, source_target_pairs={{0,1},{1,2},{2,3},{3,0},{4,5},{5,6},{6,7},{7,4},{8,9},{9,10},{10,1... | collective-permute-start | bytes 3538952 | tf_op jit(solution)/shard_map/ppermute | solution.py:51
  206.8 20.1 %copy-start.3 = (bf16[384,1536]{1,0:T(8,128)(2,1)S(1)}, bf16[384,1536]{1,0:T(8,128)(2,1)}, u32[]{:S(2)}) copy-start(bf16[384,1536]{1,0:T(8,128)(2,1)} %param.14) | copy-start | bytes 3538948
  224.1 5.6 %copy-start.5 = (bf16[384,1536]{1,0:T(8,128)(2,1)S(1)}, bf16[384,1536]{1,0:T(8,128)(2,1)}, u32[]{:S(2)}) copy-start(bf16[384,1536]{1,0:T(8,128)(2,1)} %copy-done.4) | copy-start | bytes 3538948
  229.7 5.0 %slice-start = ((s8[6291456]{0:T(1024)(128)(4,1)}), s8[4194304]{0:T(1024)(128)(4,1)S(1)}, s32[]{:S(2)}) async-start(s8[6291456]{0:T(1024)(128)(4,1)} %bitcast.84), calls=%async_computation.7 | async-start | bytes 8388608
  229.9 4.8 %copy-start.6 = (bf16[3072,1536]{1,0:T(8,128)(2,1)}, bf16[3072,1536]{1,0:T(8,128)(2,1)S(1)}, u32[]{:S(2)}) copy-start(bf16[3072,1536]{1,0:T(8,128)(2,1)S(1)} %constant_dynamic-update-slice_fusion) | copy-start | bytes 28311556
  229.9 6.2 %slice-start.1 = ((s8[6291456]{0:T(1024)(128)(4,1)}), s8[2097152]{0:T(1024)(128)(4,1)S(1)}, s32[]{:S(2)}) async-start(s8[6291456]{0:T(1024)(128)(4,1)} %bitcast.84), calls=%async_computation.8 | async-start | bytes 4194304
  234.6 3.5 copy-start.7
  238.2 1.7 copy-start.8
  239.6 199.1 %reduce-scatter.3.cloned.1.call-start = ((), (), s32[]{:S(2)}) async-start(), calls=%async_computation.4 | async-start | bytes 7077888 | tf_op jit(solution)/shard_map/reduce_scatter | solution.py:93
  245.5 4.7 %copy-start.10 = (bf16[1,128,1536]{1,2,0:T(8,128)(2,1)S(1)}, bf16[1,128,1536]{1,2,0:T(8,128)(2,1)}, u32[]{:S(2)}) copy-start(bf16[1,128,1536]{1,2,0:T(8,128)(2,1)} %copy-done.9) | copy-start | bytes 1179652
  263.8 177.0 %copy-start.1 = (bf16[1,128,1536]{2,1,0:T(8,128)(2,1)S(1)}, bf16[1,128,1536]{2,1,0:T(8,128)(2,1)}, u32[]{:S(2)}) copy-start(bf16[1,128,1536]{2,1,0:T(8,128)(2,1)} %param.15) | copy-start | bytes 1179652
Sparse Core Ops, SparseCore 0:
  10.6 65.7 all-gather.2
  78.6 58.6 all-gather.4
  149.0 59.0 reduce-scatter.4
  239.8 78.1 all-reduce.2
  321.4 117.2 reduce-scatter.2
